TPU v7x, 512 devices: a whole 4x8x8 slice. The times are simulated.
512 devices in a mesh: dof: 64 (over z, y_lo, core), real: 8 (over y_hi, x).
Axes of the slice: x: 4, y: 8 (y_hi: 2, y_lo: 4; y = y_hi * 4 + y_lo), z: 8, core: 2. Of those that a mesh axis runs over, the one named last changes fastest.
Arguments:
- mode_panel: bfloat16 [131072, 512], P('dof'), may hold values from -0.31445312 to 0.31445312
- stiff_blocks: bfloat16 [1024, 5, 128, 128], P('dof'), as said below
- stiff_cols: int32 [1024, 5], P('dof'), may hold values from 0 to 1023, as said below
- row_blade: int32 [131072], P('dof'), may hold values from 0 to 3, as said below
- adjusted_values: float32 [512], replicated, may hold values from 4 to 24
- deviations: float32 [128, 4], P('dof'), may hold values from -0.05 to 0.05
- start_block: float32 [512, 128], P('real'), may hold values from -6 to 6
Outputs:
- projected: float32 [4, 512, 512], P(None, 'real')
- subspace: float32 [128, 512, 128], P('dof', 'real')
Inputs may be any that keep to these rules, and one draw needn't show every extreme that they name: `stiff_cols`: each block row's 5 entries are, in some order, the block row itself and the block rows two and one before and one and two after it; where one of those lies outside the grid or in another blade's rows, the block row itself stands in. `stiff_blocks`: the stiffness is symmetric and couples no two blades: the block of block row g at column c is the transpose of the block of block row c at column g, diagonal blocks are symmetric, and stand-in blocks are zero. `row_blade`: block row g belongs to the blade numbered ((g + 8) // 256) mod 4 under a fixed relabelling of the blades; so each blade owns a run of 32768 neighbouring rows, except one blade, which owns the first 31744 rows and the last 1024 rows.
All inputs are finite; a program needn't handle non-finite values.
Results may differ from a plain program's by a relative error of at most 0.003.
Values may be sent and summed in bfloat16 or wider, within the bound.
No kernel may reach another device: no remote copies, remote signals or barrier semaphores. Data moves between devices by JAX's collectives and lax.ppermute only.
A program may use at most 64 MiB of HBM per device.

v0:
```python
import jax
import jax.numpy as jnp
from jax import lax
from jax.experimental import pallas as pl
from jax.experimental.pallas import tpu as pltpu
from jax.sharding import Mesh
from jax.sharding import PartitionSpec as P

MODES = 512
S = 128
BS = 128
NBR = 5
NBLADE = 4
STEPS = 2
SHARD = 16
OWN = 64
HIGHEST = lax.Precision.HIGHEST
F32 = jnp.float32
BF16 = jnp.bfloat16

DOF = ("zh", "zl", "yl", "co")
REAL = ("yh", "xx")


def dof_index():
    return lax.axis_index(DOF)


def real_index():
    return lax.axis_index(REAL)


def in_vmem(x):
    return pltpu.with_memory_space_constraint(x, pltpu.VMEM)


def in_hbm(x):
    return pltpu.with_memory_space_constraint(x, pltpu.HBM)


def image_pair(stiff_ref, panel_ref, cols_ref, row_in_ref, row, shift):
    images = []
    for t in range(2):
        blocks = jnp.concatenate([stiff_ref[row_in_ref + t, n] for n in range(NBR)], axis=1)
        picked = jnp.concatenate(
            [panel_ref[cols_ref[n, row + t] - shift] for n in range(NBR)], axis=0
        )
        images.append(jnp.dot(blocks, picked, preferred_element_type=F32).astype(BF16))
    return jnp.concatenate(images, axis=0)


def project(left, image):
    return lax.dot_general(left, image, (((0,), (0,)), ((), ())), preferred_element_type=F32)


def inner_kernel(cols_ref, stiff_hbm, panel_hbm, halves_ref, panel_ref, stiff_ref, panel_sem, stiff_sem):
    lanes = pl.ds(pl.multiple_of(real_index() // 2 * 128, 128), 128)
    first = dof_index() * SHARD
    panel_copies = [
        pltpu.make_async_copy(
            panel_hbm.at[4 * i : 4 * i + 4], panel_ref.at[4 * i : 4 * i + 4], panel_sem.at[i]
        )
        for i in range(4)
    ]
    stiff_copies = {
        q: pltpu.make_async_copy(
            stiff_hbm.at[2 * q : 2 * q + 2], stiff_ref.at[2 * q : 2 * q + 2], stiff_sem.at[q]
        )
        for q in (1, 2, 3, 4, 5, 6, 0, 7)
    }
    for copy in panel_copies:
        copy.start()
    for copy in stiff_copies.values():
        copy.start()
    for copy in panel_copies:
        copy.wait()
    for half in range(2):
        total = None
        for q in range(1 + 3 * half, 4 + 3 * half):
            stiff_copies[q].wait()
            row = 2 * q
            image = image_pair(stiff_ref, panel_ref, cols_ref, row, row, first)
            part = project(columns_pair(panel_ref, row, lanes), image)
            total = part if total is None else total + part
        halves_ref[half] = total
    stiff_copies[0].wait()
    stiff_copies[7].wait()


def columns_pair(panel_ref, row, lanes):
    return jnp.concatenate([panel_ref[row, :, lanes], panel_ref[row + 1, :, lanes]], axis=0)


def inner_rows(cols, stiff, panel):
    vmem = pl.BlockSpec(memory_space=pltpu.VMEM)
    hbm = pl.BlockSpec(memory_space=pltpu.HBM)
    return pl.pallas_call(
        inner_kernel,
        in_specs=[pl.BlockSpec(memory_space=pltpu.SMEM), hbm, hbm],
        out_specs=(vmem, vmem, vmem),
        out_shape=(
            pltpu.VMEM((2, BS, MODES), F32),
            pltpu.VMEM((SHARD, BS, MODES), BF16),
            pltpu.VMEM((SHARD, NBR, BS, BS), BF16),
        ),
        scratch_shapes=[pltpu.SemaphoreType.DMA((4,)), pltpu.SemaphoreType.DMA((8,))],
        name="inner_rows",
        compiler_params=pltpu.CompilerParams(vmem_limit_bytes=24 << 20),
    )(cols, in_hbm(stiff), in_hbm(panel))


def edge_kernel(cols_ref, stiff_ref, panel_ref, low, high, halves, out_ref, near, total):
    lanes = pl.ds(pl.multiple_of(real_index() // 2 * 128, 128), 128)
    dof = dof_index()
    last = dof % 16 == 15
    near[0, 0:2] = low[...]
    near[0, 2:6] = panel_ref[0:4]
    near[1, 0:4] = panel_ref[12:16]
    near[1, 4:6] = high[...]
    totals = []
    for side, (row, shift) in enumerate(((0, -2), (14, 12))):
        image = image_pair(stiff_ref, near.at[side], cols_ref, row, row, shift + dof * SHARD)
        totals.append(halves[side] + project(columns_pair(panel_ref, row, lanes), image))
    zero = jnp.zeros_like(totals[1])
    total[0] = totals[0] + jnp.where(last, zero, totals[1])
    total[1] = jnp.where(last, totals[1], zero)
    start = pl.multiple_of(real_index() % 2 * OWN, OWN)
    for j in range(SHARD):
        a, h = j // 2, j % 2
        for kind in range(2):
            out_ref[j, kind] = total[
                kind, pl.ds(pl.multiple_of(start + 8 * a, 8), 8), 256 * h : 256 * (h + 1)
            ]


def edge_rows(cols, stiff, panel, low, high, halves):
    vmem = pl.BlockSpec(memory_space=pltpu.VMEM)
    return pl.pallas_call(
        edge_kernel,
        in_specs=[pl.BlockSpec(memory_space=pltpu.SMEM)] + [vmem] * 5,
        out_specs=vmem,
        out_shape=jax.ShapeDtypeStruct((SHARD, 2, 8, 256), F32),
        scratch_shapes=[pltpu.VMEM((2, 6, BS, MODES), BF16), pltpu.VMEM((2, BS, MODES), F32)],
        name="edge_rows",
        compiler_params=pltpu.CompilerParams(vmem_limit_bytes=24 << 20),
    )(cols, *(in_vmem(x) for x in (stiff, panel, low, high, halves)))


def first_payload(pieces, label, start_row):
    total = jnp.sum(pieces, axis=0).reshape(16, 256)
    extra = jnp.concatenate([jnp.full((1, 256), label, F32), jnp.tile(start_row, 2)[None]], axis=0)
    return jnp.concatenate([total, jnp.pad(extra, ((0, 6), (0, 0)))], axis=0)


def second_payload(got):
    blocks = (got[:, 0:8] + jnp.roll(got[:, 8:16], 1, axis=0)).astype(BF16).reshape(32, 256)
    rows = got[:, 17, 0:S]
    high = rows.astype(BF16)
    rest = (rows - high.astype(F32)).astype(BF16)
    labels = got[:, 16, 0].astype(jnp.int32)
    rows = jnp.pad(jnp.concatenate([high, rest], axis=1), ((0, 4), (0, 0)))
    return jnp.concatenate([blocks, rows], axis=0), labels


def both(f, *lists):
    return [f(*items) for items in zip(*lists)]


def block_factor(cols, sub):
    a = [[jnp.broadcast_to(cols[j][i : i + 1, :], (8, S)) if i >= j else None for j in range(8)] for i in range(8)]
    roots = []
    low = [[None] * 8 for _ in range(8)]
    for t in range(8):
        roots.append(lax.rsqrt(a[t][t]))
        inverse = roots[t] * roots[t]
        for i in range(t + 1, 8):
            low[i][t] = a[i][t] * inverse
        for i in range(t + 1, 8):
            for j in range(t + 1, i + 1):
                a[i][j] = a[i][j] - low[i][t] * a[j][t]
    w = [[None] * 8 for _ in range(8)]
    for i in range(8):
        for j in range(i):
            total = low[i][j]
            for k in range(j + 1, i):
                total = total + low[i][k] * w[k][j]
            w[i][j] = -total
    scaled = [[w[i][j] * roots[i] if j < i else roots[i] for j in range(i + 1)] for i in range(8)]
    return scaled


def column_of(scaled, j, sub):
    out = jnp.zeros((8, S), F32)
    for i in range(j, 8):
        out = jnp.where(sub == i, scaled[i][j], out)
    return out


def twice(x):
    return jnp.concatenate([x, x], axis=1)


def apply_block(scaled, tile, sub):
    total = None
    for j in range(8):
        term = twice(column_of(scaled, j, sub)) * jnp.broadcast_to(tile[j : j + 1, :], (8, 2 * S))
        total = term if total is None else total + term
    return total


def lane_copy(tile, at):
    return jnp.broadcast_to(tile[:, at : at + 1], (8, S))


def gram_of(panel):
    high, low = split(panel)
    left_high, left_low = high[:, 0:S], low[:, 0:S]
    tall = dot(
        jnp.concatenate([left_high, left_low, left_high], axis=0),
        jnp.concatenate([high, high, low], axis=0),
        ((0,), (0,)),
    )
    return tall


def eliminate(work, sub):
    for p in range(S // 16):
        lo = 16 * p
        zs = range(2)
        one = [work[z, lo : lo + 8, :] for z in zs]
        two = [work[z, lo + 8 : lo + 16, :] for z in zs]
        cols = [[lane_copy(one[z], lo + j) for j in range(8)] for z in zs]
        cross = [[lane_copy(two[z], lo + j) for j in range(8)] for z in zs]
        scaled = [block_factor(cols[z], sub) for z in zs]
        one = [apply_block(scaled[z], one[z], sub) for z in zs]
        for i in range(8):
            for z in zs:
                ratio = None
                for j in range(i + 1):
                    term = cross[z][j] * scaled[z][i][j]
                    ratio = term if ratio is None else ratio + term
                two[z] = two[z] - twice(ratio) * jnp.broadcast_to(one[z][i : i + 1, :], (8, 2 * S))
        cols = [[lane_copy(two[z], lo + 8 + j) for j in range(8)] for z in zs]
        scaled = [block_factor(cols[z], sub) for z in zs]
        two = [apply_block(scaled[z], two[z], sub) for z in zs]
        panels = [jnp.concatenate([one[z], two[z]], axis=0) for z in zs]
        for z in zs:
            work[z, lo : lo + 16, :] = panels[z]
        if p < S // 16 - 1:
            change = [gram_of(panels[z]) for z in zs]
            for z in zs:
                work[z, lo + 16 :, :] -= change[z][lo + 16 :, :]


def split(x):
    high = x.astype(BF16)
    return high, (x - high.astype(F32)).astype(BF16)


def dot(a, b, dims=((1,), (0,))):
    return lax.dot_general(a, b, (dims, ((), ())), preferred_element_type=F32)


def product(high, low, right):
    right_high, right_low = split(right)
    wide = dot(high, jnp.concatenate([right_high, right_low], axis=1))
    return wide[:, 0:S] + wide[:, S:] + dot(low, right_high)


def solve_kernel(
    labels_ref, dev_ref, mine, other, values, proj_ref, out_ref,
    high_ref, low_ref, start_ref, image_ref, work,
):
    core = dof_index() % 2
    yh = real_index() // 4
    xx = real_index() % 4
    scale = [[dev_ref[z, labels_ref[k]] for k in range(NBLADE)] for z in range(2)]
    hit = lax.broadcasted_iota(jnp.int32, (8, 256), 1) - lax.broadcasted_iota(jnp.int32, (8, 256), 0)
    for parts, h in ((mine, core), (other, 1 - core)):

        def piece(src, y, k):
            return parts[src, y, 8 * k : 8 * k + 8, :].astype(F32)

        lanes = pl.ds(pl.multiple_of(256 * h, 256), 256)
        diagonal = jnp.broadcast_to(values[:, lanes], (8, 256))
        for zl in range(2):
            for x in range(4):
                src = zl * 4 + x
                for y in range(2):
                    for yl in range(4):
                        row = y * 256 + x * 64 + zl * 32 + yl * 8
                        blades = [piece(src, y * 4 + yl, k) for k in range(NBLADE)]
                        diag = jnp.where(hit == row - 256 * h, diagonal, 0.0)
                        for z in range(2):
                            tile = diag
                            for k in range(NBLADE):
                                tile += scale[z][k] * blades[k]
                            high, low = split(tile)
                            high_ref[z, row : row + 8, lanes] = high
                            low_ref[z, row : row + 8, lanes] = low
                        pair = parts[src, y * 4 + yl, 32:36, :].astype(F32)
                        top = y * 256 + x * 64 + zl * 16 + yl * 4
                        start_ref[pl.ds(pl.multiple_of(top + 32 * h, 4), 4), :] = pair[:, 0:S] + pair[:, S:]
            for yl in range(4):
                for k in range(NBLADE):
                    proj_ref[labels_ref[k], zl * 32 + yl * 8 : zl * 32 + yl * 8 + 8, lanes] = (
                        piece(zl * 4 + xx, yh * 4 + yl, k)
                    )

    eye = (
        lax.broadcasted_iota(jnp.int32, (S, S), 0) == lax.broadcasted_iota(jnp.int32, (S, S), 1)
    ).astype(F32)
    sub = lax.broadcasted_iota(jnp.int32, (8, S), 0)
    own = pl.ds(pl.multiple_of((yh * 4 + xx) * OWN, OWN), OWN)
    current = [start_ref[...]] * 2
    for step in range(STEPS):
        for z in range(2):
            image = product(high_ref[z], low_ref[z], current[z])
            image_ref[z] = image
            high, low = split(image)
            wide = dot(high, jnp.concatenate([high, low], axis=1), ((0,), (0,)))
            gram = wide[:, 0:S] + wide[:, S:] + dot(low, jnp.concatenate([high, low], axis=1), ((0,), (0,)))[:, 0:S]
            work[z, :, 0:S] = gram / MODES
            work[z, :, S : 2 * S] = eye
        eliminate(work, sub)
        if step < STEPS - 1:
            images = [image_ref[z] for z in range(2)]
        else:
            images = [image_ref[z, own, :] for z in range(2)]
        for z in range(2):
            high, low = split(images[z])
            inverse_high, inverse_low = split(work[z, :, S : 2 * S])
            wide = dot(high, jnp.concatenate([inverse_high, inverse_low], axis=0), ((1,), (1,)))
            current[z] = wide[:, 0:S] + wide[:, S:] + dot(low, inverse_high, ((1,), (1,)))
    for z in range(2):
        out_ref[z] = current[z]


def solve(labels, deviations, mine, other, values):
    smem = pl.BlockSpec(memory_space=pltpu.SMEM)
    vmem = pl.BlockSpec(memory_space=pltpu.VMEM)
    return pl.pallas_call(
        solve_kernel,
        in_specs=[smem, smem] + [vmem] * 3,
        out_specs=(vmem, vmem),
        out_shape=(
            jax.ShapeDtypeStruct((NBLADE, OWN, MODES), F32),
            jax.ShapeDtypeStruct((2, OWN, S), F32),
        ),
        scratch_shapes=[
            pltpu.VMEM((2, MODES, MODES), BF16),
            pltpu.VMEM((2, MODES, MODES), BF16),
            pltpu.VMEM((MODES, S), F32),
            pltpu.VMEM((2, MODES, S), F32),
            pltpu.VMEM((2, S, 2 * S), F32),
        ],
        name="solve",
        compiler_params=pltpu.CompilerParams(vmem_limit_bytes=24 << 20),
    )(labels, deviations, in_vmem(mine), in_vmem(other), values)


def spread(x, axes, count):
    return lax.all_to_all(jnp.broadcast_to(x[None], (count,) + x.shape), axes, 0, 0)


def on_device(mode_panel, stiff_blocks, stiff_cols, row_blade, adjusted_values, deviations, start_block):
    panel = mode_panel.reshape(SHARD, BS, MODES)
    count = 64
    low = lax.ppermute(panel[SHARD - 2 :], DOF, [(i, i + 1) for i in range(count - 1)])
    high = lax.ppermute(panel[:2], DOF, [(i + 1, i) for i in range(count - 1)])
    cols = stiff_cols.T
    halves, near_panel, near_stiff = inner_rows(cols, stiff_blocks, panel)
    pieces = edge_rows(cols, near_stiff, near_panel, low, high, halves)
    pieces = lax.all_to_all(pieces, ("zl", "yl", "co"), 0, 0)
    core = lax.axis_index("co")
    zl = lax.axis_index("zl")
    row = core * 32 + zl * 16 + lax.axis_index("yl") * 4 + lax.axis_index("zh")
    start_row = lax.dynamic_slice(start_block, (row, 0), (1, S))[0]
    payload = first_payload(pieces, row_blade[0].astype(F32), start_row)
    payload, labels = second_payload(spread(payload, ("zh",), 4))
    mine = spread(spread(payload, ("yh", "yl"), 8), ("zl", "xx"), 8)
    other = lax.ppermute(mine, "co", [(0, 1), (1, 0)])
    return solve(labels, deviations, mine, other, adjusted_values[None])


def solution(mesh):
    fine = Mesh(mesh.devices.reshape(4, 2, 4, 2, 2, 4), DOF + REAL)
    in_specs = (
        P(DOF, None),
        P(DOF, None, None, None),
        P(DOF, None),
        P(DOF),
        P(),
        P(DOF, None),
        P(REAL, None),
    )
    out_specs = (P(None, REAL, None), P(DOF, REAL, None))
    return jax.shard_map(on_device, mesh=fine, in_specs=in_specs, out_specs=out_specs, check_vma=False)
```

profile of v0, /device:TPU:1, one launch (start us, length us, event | category | flops | bytes accessed | tf_op | source)
XLA Modules:
  0.0 109.6 jit_solution(5305496275135801654)
XLA Ops:
  0.6 0.0 copy-start
  0.6 1.1 fusion.6
  1.7 4.6 %collective-permute-start = (bf16[2,128,512]{2,1,0:T(8,128)(2,1)S(1)}, bf16[2,128,512]{2,1,0:T(8,128)(2,1)S(1)}, u32[]{:S(2)}, u32[]{:S(2)}) collective-permute-start(bf16[2,128,512]{2,1,0:T(8,128)(2,1)S(1)} %bitcast.20), channel_id=1, source_target_pairs={{0,8},{8,16},{16,24},{24,32},{32,40},{40,48},{48,56},{56,64},{64,7... | collective-permute-start | bytes 786440 | tf_op jit(solution)/shard_map/ppermute | solution.py:369
  6.3 5.5 %collective-permute-start.1 = (bf16[2,128,512]{2,1,0:T(8,128)(2,1)S(1)}, bf16[2,128,512]{2,1,0:T(8,128)(2,1)S(1)}, u32[]{:S(2)}, u32[]{:S(2)}) collective-permute-start(bf16[2,128,512]{2,1,0:T(8,128)(2,1)S(1)} %bitcast.19), channel_id=1, source_target_pairs={{8,0},{16,8},{24,16},{32,24},{40,32},{48,40},{56,48},{64,56},{72,6... | collective-permute-start | bytes 786440 | tf_op jit(solution)/shard_map/ppermute | solution.py:370
  11.8 0.0 copy-start.1
  11.8 0.7 copy-done.1
  12.5 5.7 %inner_rows.1 = (f32[2,128,512]{2,1,0:T(8,128)S(1)}, bf16[16,128,512]{2,1,0:T(8,128)(2,1)S(1)}, bf16[16,5,128,128]{3,2,1,0:T(8,128)(2,1)S(1)}) custom-call(s32[5,16]{1,0:T(8,128)S(1)} %bitcast.15, bf16[16,5,128,128]{3,2,1,0:T(8,128)(2,1)} %stiff_hbm.1, bf16[16,128,512]{2,1,0:T(8,128)(2,1)} %bitcast.18), custom_call_target="tpu_custom_call" | custom-call | tf_op jit(solution)/shard_map/inner_rows/pallas_call | solution.py:97
  18.2 0.0 collective-permute-done.low
  18.2 0.0 collective-permute-done.1.high
  18.2 2.4 %edge_rows.1 = f32[16,2,8,256]{3,2,1,0:T(8,128)} custom-call(s32[5,16]{1,0:T(8,128)S(1)} %bitcast.16, bf16[16,5,128,128]{3,2,1,0:T(8,128)(2,1)S(1)} %get-tuple-element.5.stiff_ref, bf16[16,128,512]{2,1,0:T(8,128)(2,1)S(1)} %get-tuple-element.6.panel_ref, bf16[2,128,512]{2,1,0:T(8,128)(2,1)S(1)} %collective-permute-done.low, ...), custom_call_target="tpu_custom_call" | custom-call | tf_op jit(solution)/shard_map/edge_rows/pallas_call | solution.py:138
  20.5 5.8 %all-to-all-start = ((f32[16,2,8,256]{3,2,1,0:T(8,128)}), f32[16,2,8,256]{3,2,1,0:T(8,128)S(1)}, u32[]{:S(2)}, u32[]{:S(2)}) async-start(f32[16,2,8,256]{3,2,1,0:T(8,128)} %edge_rows.1), calls=%async_computation | async-start | bytes 524288 | tf_op jit(solution)/shard_map/all_to_all | solution.py:374
  26.3 1.2 %slice.39 = s32[1]{0:T(128)} slice(s32[2048]{0:T(1024)} %param.10), slice={[0:1]} | slice | bytes 8 | tf_op jit(solution)/shard_map/slice | solution.py:379
  28.2 0.0 copy-done
  28.2 7.6 %all-to-all-done = f32[16,2,8,256]{3,2,1,0:T(8,128)S(1)} async-done(((f32[16,2,8,256]{3,2,1,0:T(8,128)}), f32[16,2,8,256]{3,2,1,0:T(8,128)S(1)}, u32[]{:S(2)}, u32[]{:S(2)}) %all-to-all-start) | async-done | bytes 262176 | tf_op jit(solution)/shard_map/all_to_all | solution.py:374
  35.9 15.6 %all_to_all.20 = f32[4,24,256]{2,1,0:T(8,128)S(1)} all-to-all(f32[4,24,256]{2,1,0:T(8,128)S(1)} %broadcast_in_dim.8), channel_id=1, replica_groups=mesh['zh'=4,'zl'=2,'yl'=4,'co'=2,'yh'=2,'xx'=4] {'zh'}, dimensions={0} | all-to-all | bytes 196608 | tf_op jit(solution)/shard_map/all_to_all | solution.py:363
  51.6 15.0 %all_to_all.21 = bf16[8,40,256]{2,1,0:T(8,128)(2,1)S(1)} all-to-all(bf16[8,40,256]{2,1,0:T(8,128)(2,1)S(1)} %broadcast_in_dim.9), channel_id=1, replica_groups=mesh['zh'=4,'zl'=2,'yl'=4,'co'=2,'yh'=2,'xx'=4] {'yh','yl'}, dimensions={0} | all-to-all | bytes 327680 | tf_op jit(solution)/shard_map/all_to_all | solution.py:363
  66.6 0.0 copy-start.2
  66.6 0.0 copy-start.3
  66.6 0.1 broadcast_in_dim.10
  66.7 18.0 %all_to_all.22.mine = bf16[8,8,40,256]{3,2,1,0:T(8,128)(2,1)S(1)} all-to-all(bf16[8,8,40,256]{3,2,1,0:T(8,128)(2,1)S(1)} %broadcast_in_dim.10), channel_id=1, replica_groups=mesh['zh'=4,'zl'=2,'yl'=4,'co'=2,'yh'=2,'xx'=4] {'zl','xx'}, dimensions={0} | all-to-all | bytes 2621440 | tf_op jit(solution)/shard_map/all_to_all | solution.py:363
  84.7 7.4 %collective-permute-start.2 = (bf16[8,8,40,256]{3,2,1,0:T(8,128)(2,1)S(1)}, bf16[8,8,40,256]{3,2,1,0:T(8,128)(2,1)S(1)}, u32[]{:S(2)}, u32[]{:S(2)}) collective-permute-start(bf16[8,8,40,256]{3,2,1,0:T(8,128)(2,1)S(1)} %all_to_all.22.mine), channel_id=1, source_target_pairs={{0,8},{8,0},{1,9},{9,1},{2,10},{10,2},{3,11},{11,3},{4,12},{12,4},... | collective-permute-start | bytes 3932168 | tf_op jit(solution)/shard_map/ppermute | solution.py:382
  92.1 0.2 fusion.5.labels_ref
  92.3 2.3 %collective-permute-done.2.other = bf16[8,8,40,256]{3,2,1,0:T(8,128)(2,1)S(1)} collective-permute-done((bf16[8,8,40,256]{3,2,1,0:T(8,128)(2,1)S(1)}, bf16[8,8,40,256]{3,2,1,0:T(8,128)(2,1)S(1)}, u32[]{:S(2)}, u32[]{:S(2)}) %collective-permute-start.2) | collective-permute-done | bytes 1310752 | tf_op jit(solution)/shard_map/ppermute | solution.py:382
  94.6 0.0 copy-done.2
  94.6 0.0 copy-done.3
  94.6 15.0 %solve.1 = (f32[4,64,512]{2,1,0:T(8,128)}, f32[2,64,128]{2,1,0:T(8,128)}) custom-call(s32[4]{0:T(128)S(1)} %fusion.5.labels_ref, f32[2,4]{1,0:T(2,128)S(1)} %copy-done.3, bf16[8,8,40,256]{3,2,1,0:T(8,128)(2,1)S(1)} %all_to_all.22.mine, bf16[8,8,40,256]{3,2,1,0:T(8,128)(2,1)S(1)} %collective-permute-done.2.other, f32[1,512]{1,0:T(1,128)S(1)} %bitcast.17), custom_call_target="tpu_custom_call" | custom-call | tf_op jit(solution)/shard_map/solve/pallas_call | solution.py:342
  (14 shorter events, 0.1 us)
Async XLA Ops:
  0.6 27.6 %copy-start = (f32[64,128]{1,0:T(8,128)S(1)}, f32[64,128]{1,0:T(8,128)}, u32[]{:S(2)}) copy-start(f32[64,128]{1,0:T(8,128)} %param.13) | copy-start | bytes 98308
  1.7 16.4 %collective-permute-start = (bf16[2,128,512]{2,1,0:T(8,128)(2,1)S(1)}, bf16[2,128,512]{2,1,0:T(8,128)(2,1)S(1)}, u32[]{:S(2)}, u32[]{:S(2)}) collective-permute-start(bf16[2,128,512]{2,1,0:T(8,128)(2,1)S(1)} %bitcast.20), channel_id=1, source_target_pairs={{0,8},{8,16},{16,24},{24,32},{32,40},{40,48},{48,56},{56,64},{64,7... | collective-permute-start | bytes 786440 | tf_op jit(solution)/shard_map/ppermute | solution.py:369
  6.3 11.9 %collective-permute-start.1 = (bf16[2,128,512]{2,1,0:T(8,128)(2,1)S(1)}, bf16[2,128,512]{2,1,0:T(8,128)(2,1)S(1)}, u32[]{:S(2)}, u32[]{:S(2)}) collective-permute-start(bf16[2,128,512]{2,1,0:T(8,128)(2,1)S(1)} %bitcast.19), channel_id=1, source_target_pairs={{8,0},{16,8},{24,16},{32,24},{40,32},{48,40},{56,48},{64,56},{72,6... | collective-permute-start | bytes 786440 | tf_op jit(solution)/shard_map/ppermute | solution.py:370
  11.8 0.7 copy-start.1
  20.5 15.3 %all-to-all-start = ((f32[16,2,8,256]{3,2,1,0:T(8,128)}), f32[16,2,8,256]{3,2,1,0:T(8,128)S(1)}, u32[]{:S(2)}, u32[]{:S(2)}) async-start(f32[16,2,8,256]{3,2,1,0:T(8,128)} %edge_rows.1), calls=%async_computation | async-start | bytes 524288 | tf_op jit(solution)/shard_map/all_to_all | solution.py:374
  66.6 28.0 %copy-start.2 = (f32[512]{0:T(512)S(1)}, f32[512]{0:T(512)}, u32[]{:S(2)}) copy-start(f32[512]{0:T(512)} %param.11) | copy-start | bytes 6148
  66.6 28.0 %copy-start.3 = (f32[2,4]{1,0:T(2,128)S(1)}, f32[2,4]{1,0:T(2,128)}, u32[]{:S(2)}) copy-start(f32[2,4]{1,0:T(2,128)} %dev_ref.1) | copy-start | bytes 100
  84.7 9.9 %collective-permute-start.2 = (bf16[8,8,40,256]{3,2,1,0:T(8,128)(2,1)S(1)}, bf16[8,8,40,256]{3,2,1,0:T(8,128)(2,1)S(1)}, u32[]{:S(2)}, u32[]{:S(2)}) collective-permute-start(bf16[8,8,40,256]{3,2,1,0:T(8,128)(2,1)S(1)} %all_to_all.22.mine), channel_id=1, source_target_pairs={{0,8},{8,0},{1,9},{9,1},{2,10},{10,2},{3,11},{11,3},{4,12},{12,4},... | collective-permute-start | bytes 3932168 | tf_op jit(solution)/shard_map/ppermute | solution.py:382
where the time goes:
time: 110 us
  blocking collectives  48.7 us (44%)
  starting transfers between devices  23.2 us (21%)
  Pallas kernels  23 us (21%)
  waiting for transfers between devices  9.91 us (9%)
  local copies, waits for them, and re-layouts  3.1 us (3%)
  between operations  1.45 us (1%)
    all_to_all x3, blocking collectives, spread(): lax.all_to_all(jnp.broadcast_to(x[None], (count,) + x.shape), axes, 0, 0)  48.7 us
    pallas_call x1, Pallas kernels, solve(): pl.pallas_call(solve_kernel, in_specs=[smem, smem] + [vmem] * 3, out_spec...  15 us
    all_to_all x1, waiting for transfers between devices, on_device(): pieces = lax.all_to_all(pieces, ('zl', 'yl', 'co'), 0, 0)  7.61 us
    ppermute x1, starting transfers between devices, on_device(): other = lax.ppermute(mine, 'co', [(0, 1), (1, 0)])  7.4 us
    all_to_all x1, starting transfers between devices, on_device(): pieces = lax.all_to_all(pieces, ('zl', 'yl', 'co'), 0, 0)  5.79 us
    pallas_call x1, Pallas kernels, inner_rows(): pl.pallas_call(inner_kernel, in_specs=[pl.BlockSpec(memory_space=pltpu.SM...  5.67 us
    ppermute x1, starting transfers between devices, on_device(): high = lax.ppermute(panel[:2], DOF, [(i + 1, i) for i in range(count - 1)])  5.47 us
    ppermute x1, starting transfers between devices, on_device(): lax.ppermute(panel[SHARD - 2:], DOF, [(i, i + 1) for i in range(count - 1)])  4.58 us
  transfers between devices with their start and end apart: 4, of which 2 were waited for; matrix products, arithmetic and copies ran while one was open for 1% of the time, Pallas kernels for 5%

commit v1 on v0

--- a/solution.py
+++ b/solution.py
@@ -261,102 +261,133 @@
     return lax.dot_general(a, b, (dims, ((), ())), preferred_element_type=F32)
 
 
-def product(high, low, right):
-    right_high, right_low = split(right)
-    wide = dot(high, jnp.concatenate([right_high, right_low], axis=1))
-    return wide[:, 0:S] + wide[:, S:] + dot(low, right_high)
-
-
-def solve_kernel(
-    labels_ref, dev_ref, mine, other, values, proj_ref, out_ref,
-    high_ref, low_ref, start_ref, image_ref, work,
-):
-    core = dof_index() % 2
+def product(halves, right_ref, z):
+    total = None
+    for high_ref, low_ref, first in halves:
+        right_high, right_low = split(right_ref[pl.ds(pl.multiple_of(first, 256), 256), :])
+        wide = dot(high_ref[z], jnp.concatenate([right_high, right_low], axis=1))
+        part = wide[:, 0:S] + wide[:, S:] + dot(low_ref[z], right_high)
+        total = part if total is None else total + part
+    return total
+
+
+def build(labels_ref, dev_ref, parts, values, h, high_ref, low_ref, start_ref, proj_ref):
     yh = real_index() // 4
     xx = real_index() % 4
     scale = [[dev_ref[z, labels_ref[k]] for k in range(NBLADE)] for z in range(2)]
     hit = lax.broadcasted_iota(jnp.int32, (8, 256), 1) - lax.broadcasted_iota(jnp.int32, (8, 256), 0)
-    for parts, h in ((mine, core), (other, 1 - core)):
-
-        def piece(src, y, k):
-            return parts[src, y, 8 * k : 8 * k + 8, :].astype(F32)
-
-        lanes = pl.ds(pl.multiple_of(256 * h, 256), 256)
-        diagonal = jnp.broadcast_to(values[:, lanes], (8, 256))
-        for zl in range(2):
-            for x in range(4):
-                src = zl * 4 + x
-                for y in range(2):
-                    for yl in range(4):
-                        row = y * 256 + x * 64 + zl * 32 + yl * 8
-                        blades = [piece(src, y * 4 + yl, k) for k in range(NBLADE)]
-                        diag = jnp.where(hit == row - 256 * h, diagonal, 0.0)
-                        for z in range(2):
-                            tile = diag
-                            for k in range(NBLADE):
-                                tile += scale[z][k] * blades[k]
-                            high, low = split(tile)
-                            high_ref[z, row : row + 8, lanes] = high
-                            low_ref[z, row : row + 8, lanes] = low
-                        pair = parts[src, y * 4 + yl, 32:36, :].astype(F32)
-                        top = y * 256 + x * 64 + zl * 16 + yl * 4
-                        start_ref[pl.ds(pl.multiple_of(top + 32 * h, 4), 4), :] = pair[:, 0:S] + pair[:, S:]
-            for yl in range(4):
-                for k in range(NBLADE):
-                    proj_ref[labels_ref[k], zl * 32 + yl * 8 : zl * 32 + yl * 8 + 8, lanes] = (
-                        piece(zl * 4 + xx, yh * 4 + yl, k)
-                    )
+    lanes = pl.ds(pl.multiple_of(256 * h, 256), 256)
+    diagonal = jnp.broadcast_to(values[:, lanes], (8, 256))
+
+    def piece(src, y, k):
+        return parts[src, pl.ds(pl.multiple_of(32 * y + 8 * k, 8), 8), :].astype(F32)
+
+    for zl in range(2):
+        for x in range(4):
+            src = zl * 4 + x
+            for y in range(2):
+                for yl in range(4):
+                    row = y * 256 + x * 64 + zl * 32 + yl * 8
+                    blades = [piece(src, y * 4 + yl, k) for k in range(NBLADE)]
+                    diag = jnp.where(hit == row - 256 * h, diagonal, 0.0)
+                    for z in range(2):
+                        tile = diag
+                        for k in range(NBLADE):
+                            tile += scale[z][k] * blades[k]
+                        high, low = split(tile)
+                        high_ref[z, row : row + 8, :] = high
+                        low_ref[z, row : row + 8, :] = low
+                top = y * 128 + x * 32 + zl * 16
+                pair = parts[src, 256 + 16 * y : 272 + 16 * y, :].astype(F32)
+                start_ref[top : top + 16, :] = pair[:, 0:S] + pair[:, S:]
+        for yl in range(4):
+            for k in range(NBLADE):
+                at = zl * 32 + yl * 8
+                proj_ref[labels_ref[k], at : at + 8, :] = piece(zl * 4 + xx, yh * 4 + yl, k)
+
+
+def prepare_kernel(labels_ref, dev_ref, mine, values, *outs):
+    build(labels_ref, dev_ref, mine, values, dof_index() % 2, *outs)
+
+
+HALF = (
+    pltpu.VMEM((2, MODES, 256), BF16),
+    pltpu.VMEM((2, MODES, 256), BF16),
+    pltpu.VMEM((256, S), F32),
+    pltpu.VMEM((NBLADE, OWN, 256), F32),
+)
+SMEM_SPEC = pl.BlockSpec(memory_space=pltpu.SMEM)
+VMEM_SPEC = pl.BlockSpec(memory_space=pltpu.VMEM)
+
+
+def prepare(labels, deviations, mine, values):
+    return pl.pallas_call(
+        prepare_kernel,
+        in_specs=[SMEM_SPEC] * 2 + [VMEM_SPEC] * 2,
+        out_specs=(VMEM_SPEC,) * 4,
+        out_shape=HALF,
+        name="prepare",
+        compiler_params=pltpu.CompilerParams(vmem_limit_bytes=24 << 20),
+    )(labels, deviations, in_vmem(mine), values)
+
+
+def solve_kernel(
+    labels_ref, dev_ref, other, values, mine_high, mine_low, mine_start, mine_proj,
+    proj_ref, out_ref, high_ref, low_ref, half_start, half_proj, start_ref, image_ref, work,
+):
+    core = dof_index() % 2
+    build(labels_ref, dev_ref, other, values, 1 - core, high_ref, low_ref, half_start, half_proj)
+    for start, proj, h in ((mine_start, mine_proj, core), (half_start, half_proj, 1 - core)):
+        for block in range(8):
+            rows = pl.ds(pl.multiple_of(64 * block + 32 * h, 32), 32)
+            start_ref[rows, :] = start[32 * block : 32 * block + 32, :]
+        proj_ref[:, :, pl.ds(pl.multiple_of(256 * h, 256), 256)] = proj[...]
+    halves = ((mine_high, mine_low, 256 * core), (high_ref, low_ref, 256 * (1 - core)))
 
     eye = (
         lax.broadcasted_iota(jnp.int32, (S, S), 0) == lax.broadcasted_iota(jnp.int32, (S, S), 1)
     ).astype(F32)
     sub = lax.broadcasted_iota(jnp.int32, (8, S), 0)
-    own = pl.ds(pl.multiple_of((yh * 4 + xx) * OWN, OWN), OWN)
-    current = [start_ref[...]] * 2
+    own = pl.ds(pl.multiple_of(real_index() * OWN, OWN), OWN)
     for step in range(STEPS):
         for z in range(2):
-            image = product(high_ref[z], low_ref[z], current[z])
+            image = product(halves, start_ref if step == 0 else image_ref.at[z], z)
             image_ref[z] = image
             high, low = split(image)
             wide = dot(high, jnp.concatenate([high, low], axis=1), ((0,), (0,)))
-            gram = wide[:, 0:S] + wide[:, S:] + dot(low, jnp.concatenate([high, low], axis=1), ((0,), (0,)))[:, 0:S]
-            work[z, :, 0:S] = gram / MODES
+            work[z, :, 0:S] = (wide[:, 0:S] + wide[:, S:] + dot(low, high, ((0,), (0,)))) / MODES
             work[z, :, S : 2 * S] = eye
         eliminate(work, sub)
-        if step < STEPS - 1:
-            images = [image_ref[z] for z in range(2)]
-        else:
-            images = [image_ref[z, own, :] for z in range(2)]
         for z in range(2):
-            high, low = split(images[z])
+            high, low = split(image_ref[z] if step < STEPS - 1 else image_ref[z, own, :])
             inverse_high, inverse_low = split(work[z, :, S : 2 * S])
             wide = dot(high, jnp.concatenate([inverse_high, inverse_low], axis=0), ((1,), (1,)))
-            current[z] = wide[:, 0:S] + wide[:, S:] + dot(low, inverse_high, ((1,), (1,)))
-    for z in range(2):
-        out_ref[z] = current[z]
+            current = wide[:, 0:S] + wide[:, S:] + dot(low, inverse_high, ((1,), (1,)))
+            if step < STEPS - 1:
+                image_ref[z] = current
+            else:
+                out_ref[z] = current
 
 
 def solve(labels, deviations, mine, other, values):
-    smem = pl.BlockSpec(memory_space=pltpu.SMEM)
-    vmem = pl.BlockSpec(memory_space=pltpu.VMEM)
+    ready = prepare(labels, deviations, mine, values)
     return pl.pallas_call(
         solve_kernel,
-        in_specs=[smem, smem] + [vmem] * 3,
-        out_specs=(vmem, vmem),
+        in_specs=[SMEM_SPEC] * 2 + [VMEM_SPEC] * 6,
+        out_specs=(VMEM_SPEC, VMEM_SPEC),
         out_shape=(
             jax.ShapeDtypeStruct((NBLADE, OWN, MODES), F32),
             jax.ShapeDtypeStruct((2, OWN, S), F32),
         ),
         scratch_shapes=[
-            pltpu.VMEM((2, MODES, MODES), BF16),
-            pltpu.VMEM((2, MODES, MODES), BF16),
+            *HALF,
             pltpu.VMEM((MODES, S), F32),
             pltpu.VMEM((2, MODES, S), F32),
             pltpu.VMEM((2, S, 2 * S), F32),
         ],
         name="solve",
         compiler_params=pltpu.CompilerParams(vmem_limit_bytes=24 << 20),
-    )(labels, deviations, in_vmem(mine), in_vmem(other), values)
+    )(labels, deviations, in_vmem(other), values, *(in_vmem(x) for x in ready))
 
 
 def spread(x, axes, count):
@@ -378,7 +409,9 @@
     start_row = lax.dynamic_slice(start_block, (row, 0), (1, S))[0]
     payload = first_payload(pieces, row_blade[0].astype(F32), start_row)
     payload, labels = second_payload(spread(payload, ("zh",), 4))
-    mine = spread(spread(payload, ("yh", "yl"), 8), ("zl", "xx"), 8)
+    ring = spread(payload, ("yh", "yl"), 8)
+    mine = jnp.concatenate([ring[:, 0:32].reshape(256, 256), ring[:, 32:36].reshape(32, 256)], axis=0)
+    mine = spread(mine, ("zl", "xx"), 8)
     other = lax.ppermute(mine, "co", [(0, 1), (1, 0)])
     return solve(labels, deviations, mine, other, adjusted_values[None])
 

time: 110 us -> 108 us (0.982)
  waiting for transfers between devices: 9.91 us -> 8.56 us
  blocking collectives: 48.7 us -> 47.5 us
    ppermute x1, waiting for transfers between devices: 2.3 us -> 0.94 us  [on_device(): other = lax.ppermute(mine, 'co', [(0, 1), (1, 0)])]
    all_to_all x3, blocking collectives: 48.7 us -> 47.5 us  [spread(): lax.all_to_all(jnp.broadcast_to(x[None], (count,) + x.shape), axes, 0, 0)]
    pallas_call x1 -> x2, Pallas kernels: 15 us -> 15.6 us  [the longest x1 14.4 us: solve(): pl.pallas_call(solve_kernel, in_specs=[SMEM_SPEC] * 2 + [VMEM_SPEC] * 6,...]
  transfers between devices with their start and end apart: 4 -> 4, of which waited for: 2 -> 2; matrix products, arithmetic and copies ran while one was open for 1% -> 1% of each run, Pallas kernels for 5% -> 6%
where the time goes in v1:
time: 108 us
  blocking collectives  47.5 us (44%)
  Pallas kernels  23.6 us (22%)
  starting transfers between devices  23 us (21%)
  waiting for transfers between devices  8.56 us (8%)
  local copies, waits for them, and re-layouts  3.13 us (3%)
  between operations  1.51 us (1%)
    all_to_all x3, blocking collectives, spread(): lax.all_to_all(jnp.broadcast_to(x[None], (count,) + x.shape), axes, 0, 0)  47.5 us
    pallas_call x1, Pallas kernels, solve(): pl.pallas_call(solve_kernel, in_specs=[SMEM_SPEC] * 2 + [VMEM_SPEC] * 6,...  14.4 us
    all_to_all x1, waiting for transfers between devices, on_device(): pieces = lax.all_to_all(pieces, ('zl', 'yl', 'co'), 0, 0)  7.61 us
    ppermute x1, starting transfers between devices, on_device(): other = lax.ppermute(mine, 'co', [(0, 1), (1, 0)])  7.16 us
    all_to_all x1, starting transfers between devices, on_device(): pieces = lax.all_to_all(pieces, ('zl', 'yl', 'co'), 0, 0)  5.79 us
    pallas_call x1, Pallas kernels, inner_rows(): pl.pallas_call(inner_kernel, in_specs=[pl.BlockSpec(memory_space=pltpu.SM...  5.67 us
    ppermute x1, starting transfers between devices, on_device(): high = lax.ppermute(panel[:2], DOF, [(i + 1, i) for i in range(count - 1)])  5.47 us
    ppermute x1, starting transfers between devices, on_device(): lax.ppermute(panel[SHARD - 2:], DOF, [(i, i + 1) for i in range(count - 1)])  4.58 us
  transfers between devices with their start and end apart: 4, of which 2 were waited for; matrix products, arithmetic and copies ran while one was open for 1% of the time, Pallas kernels for 6%

profile of v1, /device:TPU:1, one launch (start us, length us, event | category | flops | bytes accessed | tf_op | source)
XLA Modules:
  0.0 107.5 jit_solution(1149375760363285813)
XLA Ops:
  0.6 0.0 copy-start
  0.6 1.1 fusion.6
  1.7 4.6 %collective-permute-start = (bf16[2,128,512]{2,1,0:T(8,128)(2,1)S(1)}, bf16[2,128,512]{2,1,0:T(8,128)(2,1)S(1)}, u32[]{:S(2)}, u32[]{:S(2)}) collective-permute-start(bf16[2,128,512]{2,1,0:T(8,128)(2,1)S(1)} %bitcast.23), channel_id=1, source_target_pairs={{0,8},{8,16},{16,24},{24,32},{32,40},{40,48},{48,56},{56,64},{64,7... | collective-permute-start | bytes 786440 | tf_op jit(solution)/shard_map/ppermute | solution.py:400
  6.3 5.5 %collective-permute-start.1 = (bf16[2,128,512]{2,1,0:T(8,128)(2,1)S(1)}, bf16[2,128,512]{2,1,0:T(8,128)(2,1)S(1)}, u32[]{:S(2)}, u32[]{:S(2)}) collective-permute-start(bf16[2,128,512]{2,1,0:T(8,128)(2,1)S(1)} %bitcast.22), channel_id=1, source_target_pairs={{8,0},{16,8},{24,16},{32,24},{40,32},{48,40},{56,48},{64,56},{72,6... | collective-permute-start | bytes 786440 | tf_op jit(solution)/shard_map/ppermute | solution.py:401
  11.8 0.0 copy-start.1
  11.8 0.7 copy-done.1
  12.5 5.7 %inner_rows.1 = (f32[2,128,512]{2,1,0:T(8,128)S(1)}, bf16[16,128,512]{2,1,0:T(8,128)(2,1)S(1)}, bf16[16,5,128,128]{3,2,1,0:T(8,128)(2,1)S(1)}) custom-call(s32[5,16]{1,0:T(8,128)S(1)} %bitcast.16, bf16[16,5,128,128]{3,2,1,0:T(8,128)(2,1)} %stiff_hbm.1, bf16[16,128,512]{2,1,0:T(8,128)(2,1)} %bitcast.20), custom_call_target="tpu_custom_call" | custom-call | tf_op jit(solution)/shard_map/inner_rows/pallas_call | solution.py:97
  18.2 0.0 collective-permute-done.low
  18.2 0.0 collective-permute-done.1.high
  18.2 2.4 %edge_rows.1 = f32[16,2,8,256]{3,2,1,0:T(8,128)} custom-call(s32[5,16]{1,0:T(8,128)S(1)} %bitcast.17, bf16[16,5,128,128]{3,2,1,0:T(8,128)(2,1)S(1)} %get-tuple-element.9.stiff_ref, bf16[16,128,512]{2,1,0:T(8,128)(2,1)S(1)} %get-tuple-element.10.panel_ref, bf16[2,128,512]{2,1,0:T(8,128)(2,1)S(1)} %collective-permute-done.low, ...), custom_call_target="tpu_custom_call" | custom-call | tf_op jit(solution)/shard_map/edge_rows/pallas_call | solution.py:138
  20.5 5.8 %all-to-all-start = ((f32[16,2,8,256]{3,2,1,0:T(8,128)}), f32[16,2,8,256]{3,2,1,0:T(8,128)S(1)}, u32[]{:S(2)}, u32[]{:S(2)}) async-start(f32[16,2,8,256]{3,2,1,0:T(8,128)} %edge_rows.1), calls=%async_computation | async-start | bytes 524288 | tf_op jit(solution)/shard_map/all_to_all | solution.py:405
  26.3 1.2 %slice.45 = s32[1]{0:T(128)} slice(s32[2048]{0:T(1024)} %param.10), slice={[0:1]} | slice | bytes 8 | tf_op jit(solution)/shard_map/slice | solution.py:410
  28.2 0.0 copy-done
  28.2 7.6 %all-to-all-done = f32[16,2,8,256]{3,2,1,0:T(8,128)S(1)} async-done(((f32[16,2,8,256]{3,2,1,0:T(8,128)}), f32[16,2,8,256]{3,2,1,0:T(8,128)S(1)}, u32[]{:S(2)}, u32[]{:S(2)}) %all-to-all-start) | async-done | bytes 262176 | tf_op jit(solution)/shard_map/all_to_all | solution.py:405
  35.9 15.6 %all_to_all.20 = f32[4,24,256]{2,1,0:T(8,128)S(1)} all-to-all(f32[4,24,256]{2,1,0:T(8,128)S(1)} %broadcast_in_dim.8), channel_id=1, replica_groups=mesh['zh'=4,'zl'=2,'yl'=4,'co'=2,'yh'=2,'xx'=4] {'zh'}, dimensions={0} | all-to-all | bytes 196608 | tf_op jit(solution)/shard_map/all_to_all | solution.py:394
  51.6 15.0 %all_to_all.21 = bf16[8,40,256]{2,1,0:T(8,128)(2,1)S(1)} all-to-all(bf16[8,40,256]{2,1,0:T(8,128)(2,1)S(1)} %broadcast_in_dim.9), channel_id=1, replica_groups=mesh['zh'=4,'zl'=2,'yl'=4,'co'=2,'yh'=2,'xx'=4] {'yh','yl'}, dimensions={0} | all-to-all | bytes 327680 | tf_op jit(solution)/shard_map/all_to_all | solution.py:394
  66.7 0.0 copy-start.2
  66.7 0.0 copy-start.3
  66.7 0.1 broadcast_in_dim.10
  66.8 16.9 %all_to_all.22.mine = bf16[8,288,256]{2,1,0:T(8,128)(2,1)S(1)} all-to-all(bf16[8,288,256]{2,1,0:T(8,128)(2,1)S(1)} %broadcast_in_dim.10), channel_id=1, replica_groups=mesh['zh'=4,'zl'=2,'yl'=4,'co'=2,'yh'=2,'xx'=4] {'zl','xx'}, dimensions={0} | all-to-all | bytes 2359296 | tf_op jit(solution)/shard_map/all_to_all | solution.py:394
  83.7 7.2 %collective-permute-start.2 = (bf16[8,288,256]{2,1,0:T(8,128)(2,1)S(1)}, bf16[8,288,256]{2,1,0:T(8,128)(2,1)S(1)}, u32[]{:S(2)}, u32[]{:S(2)}) collective-permute-start(bf16[8,288,256]{2,1,0:T(8,128)(2,1)S(1)} %all_to_all.22.mine), channel_id=1, source_target_pairs={{0,8},{8,0},{1,9},{9,1},{2,10},{10,2},{3,11},{11,3},{4,12},{12,4},... | collective-permute-start | bytes 3538952 | tf_op jit(solution)/shard_map/ppermute | solution.py:415
  90.8 0.2 fusion.5.labels_ref
  91.0 0.0 copy-done.2
  91.0 0.0 copy-done.3
  91.0 1.1 %prepare.1 = (bf16[2,512,256]{2,1,0:T(8,128)(2,1)S(1)}, bf16[2,512,256]{2,1,0:T(8,128)(2,1)S(1)}, f32[256,128]{1,0:T(8,128)S(1)}, f32[4,64,256]{2,1,0:T(8,128)S(1)}) custom-call(s32[4]{0:T(128)S(1)} %fusion.5.labels_ref, f32[2,4]{1,0:T(2,128)S(1)} %copy-done.3, bf16[8,288,256]{2,1,0:T(8,128)(2,1)S(1)} %all_to_all.22.mine, f32[1,512]{1,0:T(1,128)S(1)} %bitcast.18), custom_call_target="tpu_custom_call" | custom-call | tf_op jit(solution)/shard_map/prepare/pallas_call | solution.py:324
  92.2 0.9 collective-permute-done.2.other
  93.1 14.4 %solve.1 = (f32[4,64,512]{2,1,0:T(8,128)}, f32[2,64,128]{2,1,0:T(8,128)}) custom-call(s32[4]{0:T(128)S(1)} %fusion.5.labels_ref, f32[2,4]{1,0:T(2,128)S(1)} %copy-done.3, bf16[8,288,256]{2,1,0:T(8,128)(2,1)S(1)} %collective-permute-done.2.other, f32[1,512]{1,0:T(1,128)S(1)} %bitcast.19, bf16[2,512,256]{2,1,0:T(8,128)(2,1)S(1)} %get-tuple-element.12.mine_high, ...), custom_call_target="tpu_custom_call" | custom-call | tf_op jit(solution)/shard_map/solve/pallas_call | solution.py:374
  (18 shorter events, 0.2 us)
Async XLA Ops:
  0.6 27.6 %copy-start = (f32[64,128]{1,0:T(8,128)S(1)}, f32[64,128]{1,0:T(8,128)}, u32[]{:S(2)}) copy-start(f32[64,128]{1,0:T(8,128)} %param.13) | copy-start | bytes 98308
  1.7 16.4 %collective-permute-start = (bf16[2,128,512]{2,1,0:T(8,128)(2,1)S(1)}, bf16[2,128,512]{2,1,0:T(8,128)(2,1)S(1)}, u32[]{:S(2)}, u32[]{:S(2)}) collective-permute-start(bf16[2,128,512]{2,1,0:T(8,128)(2,1)S(1)} %bitcast.23), channel_id=1, source_target_pairs={{0,8},{8,16},{16,24},{24,32},{32,40},{40,48},{48,56},{56,64},{64,7... | collective-permute-start | bytes 786440 | tf_op jit(solution)/shard_map/ppermute | solution.py:400
  6.3 11.9 %collective-permute-start.1 = (bf16[2,128,512]{2,1,0:T(8,128)(2,1)S(1)}, bf16[2,128,512]{2,1,0:T(8,128)(2,1)S(1)}, u32[]{:S(2)}, u32[]{:S(2)}) collective-permute-start(bf16[2,128,512]{2,1,0:T(8,128)(2,1)S(1)} %bitcast.22), channel_id=1, source_target_pairs={{8,0},{16,8},{24,16},{32,24},{40,32},{48,40},{56,48},{64,56},{72,6... | collective-permute-start | bytes 786440 | tf_op jit(solution)/shard_map/ppermute | solution.py:401
  11.8 0.7 copy-start.1
  20.5 15.3 %all-to-all-start = ((f32[16,2,8,256]{3,2,1,0:T(8,128)}), f32[16,2,8,256]{3,2,1,0:T(8,128)S(1)}, u32[]{:S(2)}, u32[]{:S(2)}) async-start(f32[16,2,8,256]{3,2,1,0:T(8,128)} %edge_rows.1), calls=%async_computation | async-start | bytes 524288 | tf_op jit(solution)/shard_map/all_to_all | solution.py:405
  66.7 24.3 %copy-start.2 = (f32[512]{0:T(512)S(1)}, f32[512]{0:T(512)}, u32[]{:S(2)}) copy-start(f32[512]{0:T(512)} %param.11) | copy-start | bytes 6148
  66.7 24.3 %copy-start.3 = (f32[2,4]{1,0:T(2,128)S(1)}, f32[2,4]{1,0:T(2,128)}, u32[]{:S(2)}) copy-start(f32[2,4]{1,0:T(2,128)} %dev_ref.3) | copy-start | bytes 100
  83.7 9.4 %collective-permute-start.2 = (bf16[8,288,256]{2,1,0:T(8,128)(2,1)S(1)}, bf16[8,288,256]{2,1,0:T(8,128)(2,1)S(1)}, u32[]{:S(2)}, u32[]{:S(2)}) collective-permute-start(bf16[8,288,256]{2,1,0:T(8,128)(2,1)S(1)} %all_to_all.22.mine), channel_id=1, source_target_pairs={{0,8},{8,0},{1,9},{9,1},{2,10},{10,2},{3,11},{11,3},{4,12},{12,4},... | collective-permute-start | bytes 3538952 | tf_op jit(solution)/shard_map/ppermute | solution.py:415

commit v2 on v1

--- a/solution.py
+++ b/solution.py
@@ -121,16 +121,14 @@
     for side, (row, shift) in enumerate(((0, -2), (14, 12))):
         image = image_pair(stiff_ref, near.at[side], cols_ref, row, row, shift + dof * SHARD)
         totals.append(halves[side] + project(columns_pair(panel_ref, row, lanes), image))
-    zero = jnp.zeros_like(totals[1])
-    total[0] = totals[0] + jnp.where(last, zero, totals[1])
-    total[1] = jnp.where(last, totals[1], zero)
+    total[0] = jnp.where(last, totals[1], totals[0] + totals[1])
+    total[1] = totals[0]
     start = pl.multiple_of(real_index() % 2 * OWN, OWN)
     for j in range(SHARD):
         a, h = j // 2, j % 2
+        rows = pl.ds(pl.multiple_of(start + 8 * a, 8), 8)
         for kind in range(2):
-            out_ref[j, kind] = total[
-                kind, pl.ds(pl.multiple_of(start + 8 * a, 8), 8), 256 * h : 256 * (h + 1)
-            ]
+            out_ref[kind, j] = total[kind, rows, 256 * h : 256 * (h + 1)]
 
 
 def edge_rows(cols, stiff, panel, low, high, halves):
@@ -139,7 +137,7 @@
         edge_kernel,
         in_specs=[pl.BlockSpec(memory_space=pltpu.SMEM)] + [vmem] * 5,
         out_specs=vmem,
-        out_shape=jax.ShapeDtypeStruct((SHARD, 2, 8, 256), F32),
+        out_shape=jax.ShapeDtypeStruct((2, SHARD, 8, 256), F32),
         scratch_shapes=[pltpu.VMEM((2, 6, BS, MODES), BF16), pltpu.VMEM((2, BS, MODES), F32)],
         name="edge_rows",
         compiler_params=pltpu.CompilerParams(vmem_limit_bytes=24 << 20),
@@ -147,7 +145,7 @@
 
 
 def first_payload(pieces, label, start_row):
-    total = jnp.sum(pieces, axis=0).reshape(16, 256)
+    total = jnp.concatenate([jnp.sum(pieces[:15], axis=0), pieces[15]], axis=0)
     extra = jnp.concatenate([jnp.full((1, 256), label, F32), jnp.tile(start_row, 2)[None]], axis=0)
     return jnp.concatenate([total, jnp.pad(extra, ((0, 6), (0, 0)))], axis=0)
 
@@ -402,7 +400,8 @@
     cols = stiff_cols.T
     halves, near_panel, near_stiff = inner_rows(cols, stiff_blocks, panel)
     pieces = edge_rows(cols, near_stiff, near_panel, low, high, halves)
-    pieces = lax.all_to_all(pieces, ("zl", "yl", "co"), 0, 0)
+    passed = lax.ppermute(pieces[1], DOF, [(16 * k + 15, 16 * k + 14) for k in range(4)])
+    pieces = lax.all_to_all(pieces[0] + passed, ("zl", "yl", "co"), 0, 0)
     core = lax.axis_index("co")
     zl = lax.axis_index("zl")
     row = core * 32 + zl * 16 + lax.axis_index("yl") * 4 + lax.axis_index("zh")

time: 108 us -> 108 us (level)
  starting transfers between devices: 23 us -> 26.2 us
  waiting for transfers between devices: 8.56 us -> 5.83 us
    all_to_all x1, waiting for transfers between devices: 7.61 us -> 4.88 us  [on_device(): pieces = lax.all_to_all(pieces[0] + passed, ('zl', 'yl', 'co'), 0, 0)]
    all_to_all x1, starting transfers between devices: 5.79 us -> 7.61 us  [on_device(): pieces = lax.all_to_all(pieces[0] + passed, ('zl', 'yl', 'co'), 0, 0)]
  transfers between devices with their start and end apart: 4 -> 5, of which waited for: 2 -> 2; matrix products, arithmetic and copies ran while one was open for 1% -> 1% of each run, Pallas kernels for 6% -> 6%
where the time goes in v2:
time: 108 us; the launch traced here: 107 us
  blocking collectives  46.6 us (43%)
  starting transfers between devices  26.2 us (24%)
  Pallas kernels  22.9 us (21%)
  waiting for transfers between devices  5.83 us (5%)
  local copies, waits for them, and re-layouts  3.14 us (3%)
  between operations  1.54 us (1%)
    all_to_all x3, blocking collectives, spread(): lax.all_to_all(jnp.broadcast_to(x[None], (count,) + x.shape), axes, 0, 0)  46.6 us
    pallas_call x1, Pallas kernels, solve(): pl.pallas_call(solve_kernel, in_specs=[SMEM_SPEC] * 2 + [VMEM_SPEC] * 6,...  14.4 us
    ppermute x1, starting transfers between devices, on_device(): other = lax.ppermute(mine, 'co', [(0, 1), (1, 0)])  7.87 us
    all_to_all x1, starting transfers between devices, on_device(): pieces = lax.all_to_all(pieces[0] + passed, ('zl', 'yl', 'co'), 0, 0)  7.61 us
    pallas_call x1, Pallas kernels, inner_rows(): pl.pallas_call(inner_kernel, in_specs=[pl.BlockSpec(memory_space=pltpu.SM...  5.67 us
    ppermute x1, starting transfers between devices, on_device(): high = lax.ppermute(panel[:2], DOF, [(i + 1, i) for i in range(count - 1)])  5.47 us
    all_to_all x1, waiting for transfers between devices, on_device(): pieces = lax.all_to_all(pieces[0] + passed, ('zl', 'yl', 'co'), 0, 0)  4.88 us
    ppermute x1, starting transfers between devices, on_device(): lax.ppermute(panel[SHARD - 2:], DOF, [(i, i + 1) for i in range(count - 1)])  4.58 us
  transfers between devices with their start and end apart: 5, of which 2 were waited for; matrix products, arithmetic and copies ran while one was open for 1% of the time, Pallas kernels for 6%

profile of v2, /device:TPU:1, one launch (start us, length us, event | category | flops | bytes accessed | tf_op | source)
XLA Modules:
  0.0 107.2 jit_solution(218577667359728522)
XLA Ops:
  0.6 0.0 copy-start
  0.6 1.1 fusion.7
  1.7 4.6 %collective-permute-start = (bf16[2,128,512]{2,1,0:T(8,128)(2,1)S(1)}, bf16[2,128,512]{2,1,0:T(8,128)(2,1)S(1)}, u32[]{:S(2)}, u32[]{:S(2)}) collective-permute-start(bf16[2,128,512]{2,1,0:T(8,128)(2,1)S(1)} %bitcast.30), channel_id=1, source_target_pairs={{0,8},{8,16},{16,24},{24,32},{32,40},{40,48},{48,56},{56,64},{64,7... | collective-permute-start | bytes 786440 | tf_op jit(solution)/shard_map/ppermute | solution.py:398
  6.3 5.5 %collective-permute-start.1 = (bf16[2,128,512]{2,1,0:T(8,128)(2,1)S(1)}, bf16[2,128,512]{2,1,0:T(8,128)(2,1)S(1)}, u32[]{:S(2)}, u32[]{:S(2)}) collective-permute-start(bf16[2,128,512]{2,1,0:T(8,128)(2,1)S(1)} %bitcast.29), channel_id=1, source_target_pairs={{8,0},{16,8},{24,16},{32,24},{40,32},{48,40},{56,48},{64,56},{72,6... | collective-permute-start | bytes 786440 | tf_op jit(solution)/shard_map/ppermute | solution.py:399
  11.8 0.0 copy-start.1
  11.8 0.7 copy-done.1
  12.5 5.7 %inner_rows.1 = (f32[2,128,512]{2,1,0:T(8,128)S(1)}, bf16[16,128,512]{2,1,0:T(8,128)(2,1)S(1)}, bf16[16,5,128,128]{3,2,1,0:T(8,128)(2,1)S(1)}) custom-call(s32[5,16]{1,0:T(8,128)S(1)} %bitcast.23, bf16[16,5,128,128]{3,2,1,0:T(8,128)(2,1)} %stiff_hbm.1, bf16[16,128,512]{2,1,0:T(8,128)(2,1)} %bitcast.27), custom_call_target="tpu_custom_call" | custom-call | tf_op jit(solution)/shard_map/inner_rows/pallas_call | solution.py:97
  18.2 0.0 collective-permute-done.low
  18.2 0.0 collective-permute-done.1.high
  18.2 1.7 %edge_rows.1 = f32[2,16,8,256]{3,2,1,0:T(8,128)S(1)} custom-call(s32[5,16]{1,0:T(8,128)S(1)} %bitcast.24, bf16[16,5,128,128]{3,2,1,0:T(8,128)(2,1)S(1)} %get-tuple-element.9.stiff_ref, bf16[16,128,512]{2,1,0:T(8,128)(2,1)S(1)} %get-tuple-element.10.panel_ref, bf16[2,128,512]{2,1,0:T(8,128)(2,1)S(1)} %collective-permute-done.low, ...), custom_call_target="tpu_custom_call" | custom-call | tf_op jit(solution)/shard_map/edge_rows/pallas_call | solution.py:136
  19.9 0.7 collective-permute-start.2
  20.5 0.0 collective-permute-done.2
  20.6 0.7 fusion
  21.2 7.6 %all-to-all-start = ((f32[16,8,256]{2,1,0:T(8,128)}), f32[16,8,256]{2,1,0:T(8,128)S(1)}, u32[]{:S(2)}, u32[]{:S(2)}) async-start(f32[16,8,256]{2,1,0:T(8,128)} %fusion), calls=%async_computation | async-start | bytes 262144 | tf_op jit(solution)/shard_map/all_to_all | solution.py:404
  28.8 1.2 %slice.61 = s32[1]{0:T(128)} slice(s32[2048]{0:T(1024)} %param.10), slice={[0:1]} | slice | bytes 8 | tf_op jit(solution)/shard_map/slice | solution.py:409
  30.7 0.0 copy-done
  30.7 4.9 %all-to-all-done = f32[16,8,256]{2,1,0:T(8,128)S(1)} async-done(((f32[16,8,256]{2,1,0:T(8,128)}), f32[16,8,256]{2,1,0:T(8,128)S(1)}, u32[]{:S(2)}, u32[]{:S(2)}) %all-to-all-start) | async-done | bytes 131104 | tf_op jit(solution)/shard_map/all_to_all | solution.py:404
  35.7 15.2 %all_to_all.20 = f32[4,24,256]{2,1,0:T(8,128)S(1)} all-to-all(f32[4,24,256]{2,1,0:T(8,128)S(1)} %broadcast_in_dim.8), channel_id=1, replica_groups=mesh['zh'=4,'zl'=2,'yl'=4,'co'=2,'yh'=2,'xx'=4] {'zh'}, dimensions={0} | all-to-all | bytes 196608 | tf_op jit(solution)/shard_map/all_to_all | solution.py:392
  50.9 14.9 %all_to_all.21 = bf16[8,40,256]{2,1,0:T(8,128)(2,1)S(1)} all-to-all(bf16[8,40,256]{2,1,0:T(8,128)(2,1)S(1)} %broadcast_in_dim.9), channel_id=1, replica_groups=mesh['zh'=4,'zl'=2,'yl'=4,'co'=2,'yh'=2,'xx'=4] {'yh','yl'}, dimensions={0} | all-to-all | bytes 327680 | tf_op jit(solution)/shard_map/all_to_all | solution.py:392
  65.9 0.0 copy-start.2
  65.9 0.0 copy-start.3
  65.9 0.1 broadcast_in_dim.10
  66.0 16.6 %all_to_all.22.mine = bf16[8,288,256]{2,1,0:T(8,128)(2,1)S(1)} all-to-all(bf16[8,288,256]{2,1,0:T(8,128)(2,1)S(1)} %broadcast_in_dim.10), channel_id=1, replica_groups=mesh['zh'=4,'zl'=2,'yl'=4,'co'=2,'yh'=2,'xx'=4] {'zl','xx'}, dimensions={0} | all-to-all | bytes 2359296 | tf_op jit(solution)/shard_map/all_to_all | solution.py:392
  82.6 7.9 %collective-permute-start.3 = (bf16[8,288,256]{2,1,0:T(8,128)(2,1)S(1)}, bf16[8,288,256]{2,1,0:T(8,128)(2,1)S(1)}, u32[]{:S(2)}, u32[]{:S(2)}) collective-permute-start(bf16[8,288,256]{2,1,0:T(8,128)(2,1)S(1)} %all_to_all.22.mine), channel_id=1, source_target_pairs={{0,8},{8,0},{1,9},{9,1},{2,10},{10,2},{3,11},{11,3},{4,12},{12,4},... | collective-permute-start | bytes 3538952 | tf_op jit(solution)/shard_map/ppermute | solution.py:414
  90.5 0.2 fusion.6.labels_ref
  90.6 0.0 copy-done.2
  90.6 0.0 copy-done.3
  90.6 1.1 %prepare.1 = (bf16[2,512,256]{2,1,0:T(8,128)(2,1)S(1)}, bf16[2,512,256]{2,1,0:T(8,128)(2,1)S(1)}, f32[256,128]{1,0:T(8,128)S(1)}, f32[4,64,256]{2,1,0:T(8,128)S(1)}) custom-call(s32[4]{0:T(128)S(1)} %fusion.6.labels_ref, f32[2,4]{1,0:T(2,128)S(1)} %copy-done.3, bf16[8,288,256]{2,1,0:T(8,128)(2,1)S(1)} %all_to_all.22.mine, f32[1,512]{1,0:T(1,128)S(1)} %bitcast.25), custom_call_target="tpu_custom_call" | custom-call | tf_op jit(solution)/shard_map/prepare/pallas_call | solution.py:322
  91.8 0.9 collective-permute-done.3.other
  92.7 14.4 %solve.1 = (f32[4,64,512]{2,1,0:T(8,128)}, f32[2,64,128]{2,1,0:T(8,128)}) custom-call(s32[4]{0:T(128)S(1)} %fusion.6.labels_ref, f32[2,4]{1,0:T(2,128)S(1)} %copy-done.3, bf16[8,288,256]{2,1,0:T(8,128)(2,1)S(1)} %collective-permute-done.3.other, f32[1,512]{1,0:T(1,128)S(1)} %bitcast.26, bf16[2,512,256]{2,1,0:T(8,128)(2,1)S(1)} %get-tuple-element.12.mine_high, ...), custom_call_target="tpu_custom_call" | custom-call | tf_op jit(solution)/shard_map/solve/pallas_call | solution.py:372
  (20 shorter events, 0.2 us)
Async XLA Ops:
  0.6 30.1 %copy-start = (f32[64,128]{1,0:T(8,128)S(1)}, f32[64,128]{1,0:T(8,128)}, u32[]{:S(2)}) copy-start(f32[64,128]{1,0:T(8,128)} %param.13) | copy-start | bytes 98308
  1.7 16.4 %collective-permute-start = (bf16[2,128,512]{2,1,0:T(8,128)(2,1)S(1)}, bf16[2,128,512]{2,1,0:T(8,128)(2,1)S(1)}, u32[]{:S(2)}, u32[]{:S(2)}) collective-permute-start(bf16[2,128,512]{2,1,0:T(8,128)(2,1)S(1)} %bitcast.30), channel_id=1, source_target_pairs={{0,8},{8,16},{16,24},{24,32},{32,40},{40,48},{48,56},{56,64},{64,7... | collective-permute-start | bytes 786440 | tf_op jit(solution)/shard_map/ppermute | solution.py:398
  6.3 11.9 %collective-permute-start.1 = (bf16[2,128,512]{2,1,0:T(8,128)(2,1)S(1)}, bf16[2,128,512]{2,1,0:T(8,128)(2,1)S(1)}, u32[]{:S(2)}, u32[]{:S(2)}) collective-permute-start(bf16[2,128,512]{2,1,0:T(8,128)(2,1)S(1)} %bitcast.29), channel_id=1, source_target_pairs={{8,0},{16,8},{24,16},{32,24},{40,32},{48,40},{56,48},{64,56},{72,6... | collective-permute-start | bytes 786440 | tf_op jit(solution)/shard_map/ppermute | solution.py:399
  11.8 0.7 copy-start.1
  19.9 0.7 collective-permute-start.2
  21.2 14.4 %all-to-all-start = ((f32[16,8,256]{2,1,0:T(8,128)}), f32[16,8,256]{2,1,0:T(8,128)S(1)}, u32[]{:S(2)}, u32[]{:S(2)}) async-start(f32[16,8,256]{2,1,0:T(8,128)} %fusion), calls=%async_computation | async-start | bytes 262144 | tf_op jit(solution)/shard_map/all_to_all | solution.py:404
  65.9 24.8 %copy-start.2 = (f32[512]{0:T(512)S(1)}, f32[512]{0:T(512)}, u32[]{:S(2)}) copy-start(f32[512]{0:T(512)} %param.11) | copy-start | bytes 6148
  65.9 24.8 %copy-start.3 = (f32[2,4]{1,0:T(2,128)S(1)}, f32[2,4]{1,0:T(2,128)}, u32[]{:S(2)}) copy-start(f32[2,4]{1,0:T(2,128)} %dev_ref.3) | copy-start | bytes 100
  82.6 10.1 %collective-permute-start.3 = (bf16[8,288,256]{2,1,0:T(8,128)(2,1)S(1)}, bf16[8,288,256]{2,1,0:T(8,128)(2,1)S(1)}, u32[]{:S(2)}, u32[]{:S(2)}) collective-permute-start(bf16[8,288,256]{2,1,0:T(8,128)(2,1)S(1)} %all_to_all.22.mine), channel_id=1, source_target_pairs={{0,8},{8,0},{1,9},{9,1},{2,10},{10,2},{3,11},{11,3},{4,12},{12,4},... | collective-permute-start | bytes 3538952 | tf_op jit(solution)/shard_map/ppermute | solution.py:414
